TPU v7x, 32 devices: a whole 2x2x4 slice. The times are simulated.
32 devices in a mesh: fsdp: 2 (over core), expert: 16 (over z, y, x).
Axes of the slice: x: 2, y: 2, z: 4, core: 2. Of those that a mesh axis runs over, the one named last changes fastest.
Arguments:
- tokens: bfloat16 [16, 2048, 1024], P('expert', 'fsdp'), may hold values from -6 to 6
- out_grad: bfloat16 [16, 2048, 1024], P('expert', 'fsdp'), may hold values from -8 to 8
- routes: int32 [16, 2048, 1], P('expert', 'fsdp'), may hold values from 0 to 15; in each aligned block of 1024 rows (0 to 1023, 1024 to 2047, ..., all dimensions but the last counted through in order) at most 128 rows name the same one
- prefix: int32 [16], P('expert'), may hold values from 204 to 1024
- ln1_gain: bfloat16 [1024], P('fsdp'), may hold values from 0.5 to 1.5
- ln1_bias: bfloat16 [1024], P('fsdp'), may hold values from -0.625 to 0.625
- w_qkv: bfloat16 [1024, 3072], P('fsdp'), may hold values from -0.1875 to 0.1875
- q_bias: bfloat16 [1024], P('fsdp'), may hold values from -0.625 to 0.625
- v_bias: bfloat16 [1024], P('fsdp'), may hold values from -0.625 to 0.625
- attention_output_weight: bfloat16 [1024, 1024], P('fsdp'), may hold values from -4 to 4
- attention_output_bias: bfloat16 [1024], P('fsdp'), may hold values from -0.625 to 0.625
- ln2_gain: bfloat16 [1024], P('fsdp'), may hold values from 0.5 to 1.5
- ln2_bias: bfloat16 [1024], P('fsdp'), may hold values from -0.625 to 0.625
- w_router: bfloat16 [1024, 16], P('fsdp'), may hold values from -0.09375 to 0.09375
- moe_bias: bfloat16 [1024], P('fsdp'), may hold values from -0.625 to 0.625
- w_in: bfloat16 [16, 1024, 4096], P('expert', None, 'fsdp'), may hold values from -0.1875 to 0.1875
- w_down: bfloat16 [16, 4096, 1024], P('expert', 'fsdp'), may hold values from -1.5 to 1.5
Outputs:
- out: bfloat16 [16, 2048, 1024], P('expert', 'fsdp')
- d_tokens: bfloat16 [16, 2048, 1024], P('expert', 'fsdp')
- d_ln1_gain: float32 [1024], P(('fsdp', 'expert'))
- d_ln1_bias: float32 [1024], P(('fsdp', 'expert'))
- d_w_qkv: float32 [1024, 3072], P(('fsdp', 'expert'))
- d_q_bias: float32 [1024], P(('fsdp', 'expert'))
- d_v_bias: float32 [1024], P(('fsdp', 'expert'))
- d_w_out: float32 [1024, 1024], P(('fsdp', 'expert'))
- d_out_bias: float32 [1024], P(('fsdp', 'expert'))
- d_ln2_gain: float32 [1024], P(('fsdp', 'expert'))
- d_ln2_bias: float32 [1024], P(('fsdp', 'expert'))
- d_w_router: float32 [1024, 16], P(('fsdp', 'expert'))
- d_moe_bias: float32 [1024], P(('fsdp', 'expert'))
- d_w_in: float32 [16, 1024, 4096], P('expert', None, 'fsdp')
- d_w_down: float32 [16, 4096, 1024], P('expert', 'fsdp')
Inputs may be any that keep to these rules, and one draw needn't show every extreme that they name: `routes`: in each aligned block of 1024 rows (the positions of one sequence on one device) at most 128 rows name the same expert, and some block has 128 that do.
All inputs are finite; a program needn't handle non-finite values.
Results may differ from a plain program's by a relative error of at most 0.02.
Values may be sent and summed in bfloat16 or wider, within the bound.
No kernel may reach another device: no remote copies, remote signals or barrier semaphores. Data moves between devices by JAX's collectives and lax.ppermute only.
A program may use at most 384 MiB of HBM per device.

v0:
```python
from functools import partial
import math
import jax
import jax.numpy as jnp
from jax import lax
from jax.sharding import PartitionSpec as P

HEAD_DIM = 64
NORM_EPSILON = 1e-05
MASK_FILL = -1e30


def passed_along(array, axis, by):
    size = lax.axis_size(axis)
    pairs = [(i, i + by) for i in range(size) if 0 <= i + by < size]
    return lax.ppermute(array, axis, pairs)


def layer_norm(values, norm_gain, norm_bias):
    center = values - jnp.mean(values, axis=-1, keepdims=True)
    inv_std = lax.rsqrt(jnp.mean(center * center, axis=-1, keepdims=True) + NORM_EPSILON)
    normed = center * inv_std
    return (normed * norm_gain + norm_bias, normed, inv_std)


def norm_backward(grad_out, normed, inv_std, norm_gain):
    scaled = grad_out * norm_gain
    return inv_std * (
        scaled
        - jnp.mean(scaled, axis=-1, keepdims=True)
        - normed * jnp.mean(scaled * normed, axis=-1, keepdims=True)
    )


def contract_rows(left_side, right_side):
    return lax.dot_general(
        left_side, right_side, (((0,), (0,)), ((), ())), preferred_element_type=jnp.float32
    )


def contract_last(left_side, right_side):
    return lax.dot_general(
        left_side, right_side, (((1,), (1,)), ((), ())), preferred_element_type=jnp.float32
    )


def visible(query_pos, key_pos, prefix_len):
    keys_row = key_pos[None, :]
    return ((keys_row <= query_pos[:, None]) | (keys_row < prefix_len)) & (keys_row >= 0)


def body(
    tokens,
    out_grad,
    routes,
    prefix,
    ln1_gain,
    ln1_bias,
    w_qkv,
    q_bias,
    v_bias,
    attention_output_weight,
    attention_output_bias,
    ln2_gain,
    ln2_bias,
    w_router,
    moe_bias,
    w_in,
    w_down,
):
    gathered = (
        lax.all_gather(ln1_gain, "fsdp", axis=0, tiled=True),
        lax.all_gather(ln1_bias, "fsdp", axis=0, tiled=True),
        lax.all_gather(w_qkv, "fsdp", axis=0, tiled=True),
        lax.all_gather(q_bias, "fsdp", axis=0, tiled=True),
        lax.all_gather(v_bias, "fsdp", axis=0, tiled=True),
        lax.all_gather(attention_output_weight, "fsdp", axis=0, tiled=True),
        lax.all_gather(attention_output_bias, "fsdp", axis=0, tiled=True),
        lax.all_gather(ln2_gain, "fsdp", axis=0, tiled=True),
        lax.all_gather(ln2_bias, "fsdp", axis=0, tiled=True),
        lax.all_gather(w_router, "fsdp", axis=0, tiled=True),
        lax.all_gather(moe_bias, "fsdp", axis=0, tiled=True),
    )
    qkv_weight = gathered[2]
    out_weight = gathered[5]
    router_weight = gathered[9]
    norm1_gain = gathered[0].astype(jnp.float32)
    norm1_bias = gathered[1].astype(jnp.float32)
    query_bias = gathered[3].astype(jnp.float32)
    value_bias = gathered[4].astype(jnp.float32)
    output_bias = gathered[6].astype(jnp.float32)
    norm2_gain = gathered[7].astype(jnp.float32)
    norm2_bias = gathered[8].astype(jnp.float32)
    expert_bias = gathered[10].astype(jnp.float32)
    row_count = tokens.shape[1]
    model_width = tokens.shape[2]
    head_count = model_width // HEAD_DIM
    query_scale = HEAD_DIM ** (-0.5)
    experts_all = router_weight.shape[1]
    most_slots = max(2, 2 * row_count // experts_all)
    half_index = lax.axis_index("fsdp")
    query_pos = half_index * row_count + jnp.arange(row_count, dtype=jnp.int32)
    key_pos = jnp.concatenate([query_pos - row_count, query_pos])
    prefix_len = prefix[0]
    residual = tokens[0].astype(jnp.float32)
    norm1_out, normed1, inv_std1 = layer_norm(residual, norm1_gain, norm1_bias)
    attn_in = norm1_out.astype(jnp.bfloat16)
    projected = jnp.dot(attn_in, qkv_weight, preferred_element_type=jnp.float32)
    queries = ((projected[:, :model_width] + query_bias) * query_scale).astype(jnp.bfloat16)
    key_value = jnp.concatenate(
        [projected[:, model_width : 2 * model_width], projected[:, 2 * model_width :] + value_bias],
        axis=1,
    ).astype(jnp.bfloat16)
    earlier = passed_along(key_value, "fsdp", 1)
    all_keys = jnp.concatenate([earlier, key_value], axis=0)
    query_heads = queries.reshape(row_count, head_count, HEAD_DIM)
    key_count = all_keys.shape[0]
    block_rows = math.gcd(key_count, 512)

    def key_block(block_index):
        offset = block_index * block_rows
        key_part = lax.dynamic_slice_in_dim(all_keys, offset, block_rows, 0)
        key_heads = key_part[:, :model_width].reshape(block_rows, head_count, HEAD_DIM)
        value_heads = key_part[:, model_width:].reshape(block_rows, head_count, HEAD_DIM)
        allowed = visible(
            query_pos, lax.dynamic_slice_in_dim(key_pos, offset, block_rows, 0), prefix_len
        )[None]
        return (key_heads, value_heads, allowed)

    def forward_block(carried, block_index):
        run_max, run_sum, run_acc = carried
        key_heads, value_heads, allowed = key_block(block_index)
        scores = jnp.einsum(
            "qhd,khd->hqk", query_heads, key_heads, preferred_element_type=jnp.float32
        )
        updated_maximum = jnp.maximum(
            run_max, jnp.max(jnp.where(allowed, scores, MASK_FILL), axis=-1)
        )
        weights = jnp.where(allowed, jnp.exp(scores - updated_maximum[..., None]), 0.0)
        factor = jnp.exp(run_max - updated_maximum)
        run_sum = run_sum * factor + jnp.sum(weights, axis=-1)
        run_acc = run_acc * factor[..., None] + jnp.einsum(
            "hqk,khd->hqd",
            weights.astype(jnp.bfloat16),
            value_heads,
            preferred_element_type=jnp.float32,
        )
        return ((updated_maximum, run_sum, run_acc), None)

    start_state = (
        jnp.full((head_count, row_count), MASK_FILL, jnp.float32),
        jnp.zeros((head_count, row_count), jnp.float32),
        jnp.zeros((head_count, row_count, HEAD_DIM), jnp.float32),
    )
    final_state, unused = lax.scan(forward_block, start_state, jnp.arange(key_count // block_rows))
    run_max, run_sum, run_acc = final_state
    log_sum = run_max + jnp.log(run_sum)
    context_heads = run_acc / run_sum[..., None]
    context_vectors = jnp.transpose(context_heads, (1, 0, 2)).reshape(row_count, model_width)
    context_low = context_vectors.astype(jnp.bfloat16)
    attention_result = (
        jnp.dot(context_low, out_weight, preferred_element_type=jnp.float32) + output_bias
    )
    hidden = residual + attention_result
    norm2_out, normed2, inv_std2 = layer_norm(hidden, norm2_gain, norm2_bias)
    mixed_low = norm2_out.astype(jnp.bfloat16)
    logits = jnp.dot(mixed_low, router_weight, preferred_element_type=jnp.float32)
    router_probs = jax.nn.softmax(logits, axis=-1)
    token_route = routes[0, :, 0]
    one_hot = (token_route[:, None] == jnp.arange(experts_all, dtype=jnp.int32)[None, :]).astype(
        jnp.float32
    )
    gate_value = jnp.sum(router_probs * one_hot, axis=-1)
    earlier_same = jnp.cumsum(one_hot, axis=0) - one_hot
    slot_index = jnp.sum(earlier_same * one_hot, axis=-1).astype(jnp.int32)

    def dispatch(row_values):
        empty_buffer = jnp.zeros((experts_all, most_slots, model_width), row_values.dtype)
        return empty_buffer.at[token_route, slot_index].set(row_values)

    def collect(buffer):
        return buffer[token_route, slot_index]

    arrived = lax.all_to_all(dispatch(mixed_low), "expert", split_axis=0, concat_axis=1, tiled=True)
    owner_in = lax.all_gather(arrived, "fsdp", axis=1, tiled=True)
    pre_act = jnp.einsum("erd,edh->erh", owner_in, w_in, preferred_element_type=jnp.float32)
    activation = jax.nn.gelu(pre_act, approximate=True).astype(jnp.bfloat16)
    partial_out = jnp.einsum("erh,ehd->erd", activation, w_down, preferred_element_type=jnp.float32)
    expert_rows = lax.psum_scatter(
        partial_out.astype(jnp.bfloat16), "fsdp", scatter_dimension=1, tiled=True
    )
    returned = lax.all_to_all(expert_rows, "expert", split_axis=1, concat_axis=0, tiled=True)
    expert_value = collect(returned).astype(jnp.float32)
    output = hidden + gate_value[:, None] * expert_value + expert_bias
    out_cot = out_grad[0].astype(jnp.float32)
    d_expert_bias = jnp.sum(out_cot, axis=0)
    d_gate = jnp.sum(out_cot * expert_value, axis=-1)
    d_expert_value = (gate_value[:, None] * out_cot).astype(jnp.bfloat16)
    grads_arrived = lax.all_to_all(
        dispatch(d_expert_value), "expert", split_axis=0, concat_axis=1, tiled=True
    )
    unused_out, gelu_back = jax.vjp(partial(jax.nn.gelu, approximate=True), pre_act)
    grad_in = lax.all_gather(grads_arrived, "fsdp", axis=1, tiled=True)
    d_activ = jnp.einsum("erd,ehd->erh", grad_in, w_down, preferred_element_type=jnp.float32)
    d_w_down_out = jnp.einsum(
        "erh,erd->ehd", activation, grad_in, preferred_element_type=jnp.float32
    )
    d_pre = gelu_back(d_activ)[0].astype(jnp.bfloat16)
    d_w_in_out = jnp.einsum("erd,erh->edh", owner_in, d_pre, preferred_element_type=jnp.float32)
    d_rows_part = jnp.einsum("erh,edh->erd", d_pre, w_in, preferred_element_type=jnp.float32)
    d_rows = lax.psum_scatter(
        d_rows_part.astype(jnp.bfloat16), "fsdp", scatter_dimension=1, tiled=True
    )
    d_mixed_expert = collect(
        lax.all_to_all(d_rows, "expert", split_axis=1, concat_axis=0, tiled=True)
    ).astype(jnp.float32)
    d_logits = ((d_gate * gate_value)[:, None] * (one_hot - router_probs)).astype(jnp.bfloat16)
    d_mixed = contract_last(d_logits, router_weight) + d_mixed_expert
    d_router = contract_rows(mixed_low, d_logits)
    d_norm2_gain = jnp.sum(d_mixed * normed2, axis=0)
    d_norm2_bias = jnp.sum(d_mixed, axis=0)
    d_hidden = out_cot + norm_backward(d_mixed, normed2, inv_std2, norm2_gain)
    d_attn = d_hidden.astype(jnp.bfloat16)
    d_output_bias = jnp.sum(d_attn.astype(jnp.float32), axis=0)
    d_out_weight = contract_rows(context_low, d_attn)
    d_context = contract_last(d_attn, out_weight).astype(jnp.bfloat16)
    d_context_heads = d_context.reshape(row_count, head_count, HEAD_DIM)
    row_delta = jnp.sum(
        jnp.transpose(d_context_heads.astype(jnp.float32), (1, 0, 2)) * context_heads, axis=-1
    )

    def backward_block(d_query_acc, block_index):
        key_heads, value_heads, allowed = key_block(block_index)
        scores = jnp.einsum(
            "qhd,khd->hqk", query_heads, key_heads, preferred_element_type=jnp.float32
        )
        probs_part = jnp.where(allowed, jnp.exp(scores - log_sum[..., None]), 0.0)
        d_probs = jnp.einsum(
            "qhd,khd->hqk", d_context_heads, value_heads, preferred_element_type=jnp.float32
        )
        d_scores = (probs_part * (d_probs - row_delta[..., None])).astype(jnp.bfloat16)
        d_query_acc = d_query_acc + jnp.einsum(
            "hqk,khd->qhd", d_scores, key_heads, preferred_element_type=jnp.float32
        )
        d_key_part = jnp.einsum(
            "hqk,qhd->khd", d_scores, query_heads, preferred_element_type=jnp.float32
        ).reshape(block_rows, model_width)
        d_value_part = jnp.einsum(
            "hqk,qhd->khd",
            probs_part.astype(jnp.bfloat16),
            d_context_heads,
            preferred_element_type=jnp.float32,
        ).reshape(block_rows, model_width)
        return (d_query_acc, jnp.concatenate([d_key_part, d_value_part], axis=1))

    d_query_sum, d_kv_blocks = lax.scan(
        backward_block,
        jnp.zeros((row_count, head_count, HEAD_DIM), jnp.float32),
        jnp.arange(key_count // block_rows),
    )
    d_kv_all = d_kv_blocks.reshape(key_count, 2 * model_width)
    returned_kv = passed_along(d_kv_all[:row_count].astype(jnp.bfloat16), "fsdp", -1).astype(
        jnp.float32
    )
    d_key_value = (d_kv_all[row_count:] + returned_kv).astype(jnp.bfloat16)
    d_query = (d_query_sum.reshape(row_count, model_width) * query_scale).astype(jnp.bfloat16)
    d_qkv = jnp.concatenate([d_query, d_key_value], axis=1)
    d_query_bias = jnp.sum(d_query.astype(jnp.float32), axis=0)
    d_value_bias = jnp.sum(d_key_value[:, model_width:].astype(jnp.float32), axis=0)
    query_key_value_weight_grad = contract_rows(attn_in, d_qkv)
    d_norm1_out = contract_last(d_qkv, qkv_weight)
    d_norm1_gain = jnp.sum(d_norm1_out * normed1, axis=0)
    d_norm1_bias = jnp.sum(d_norm1_out, axis=0)
    d_tokens = (d_hidden + norm_backward(d_norm1_out, normed1, inv_std1, norm1_gain)).astype(
        jnp.bfloat16
    )
    summed = (
        lax.psum_scatter(d_norm1_gain, ("fsdp", "expert"), scatter_dimension=0, tiled=True),
        lax.psum_scatter(d_norm1_bias, ("fsdp", "expert"), scatter_dimension=0, tiled=True),
        lax.psum_scatter(
            query_key_value_weight_grad, ("fsdp", "expert"), scatter_dimension=0, tiled=True
        ),
        lax.psum_scatter(d_query_bias, ("fsdp", "expert"), scatter_dimension=0, tiled=True),
        lax.psum_scatter(d_value_bias, ("fsdp", "expert"), scatter_dimension=0, tiled=True),
        lax.psum_scatter(d_out_weight, ("fsdp", "expert"), scatter_dimension=0, tiled=True),
        lax.psum_scatter(d_output_bias, ("fsdp", "expert"), scatter_dimension=0, tiled=True),
        lax.psum_scatter(d_norm2_gain, ("fsdp", "expert"), scatter_dimension=0, tiled=True),
        lax.psum_scatter(d_norm2_bias, ("fsdp", "expert"), scatter_dimension=0, tiled=True),
        lax.psum_scatter(d_router, ("fsdp", "expert"), scatter_dimension=0, tiled=True),
        lax.psum_scatter(d_expert_bias, ("fsdp", "expert"), scatter_dimension=0, tiled=True),
    )
    return (
        output.astype(jnp.bfloat16)[None],
        d_tokens[None],
        summed[0],
        summed[1],
        summed[2],
        summed[3],
        summed[4],
        summed[5],
        summed[6],
        summed[7],
        summed[8],
        summed[9],
        summed[10],
        d_w_in_out,
        d_w_down_out,
    )


def solution(mesh):
    return jax.shard_map(
        body,
        mesh=mesh,
        in_specs=(
            P("expert", "fsdp", None),
            P("expert", "fsdp", None),
            P("expert", "fsdp", None),
            P("expert"),
            P("fsdp"),
            P("fsdp"),
            P("fsdp", None),
            P("fsdp"),
            P("fsdp"),
            P("fsdp", None),
            P("fsdp"),
            P("fsdp"),
            P("fsdp"),
            P("fsdp", None),
            P("fsdp"),
            P("expert", None, "fsdp"),
            P("expert", "fsdp", None),
        ),
        out_specs=(
            P("expert", "fsdp", None),
            P("expert", "fsdp", None),
            P(("fsdp", "expert")),
            P(("fsdp", "expert")),
            P(("fsdp", "expert"), None),
            P(("fsdp", "expert")),
            P(("fsdp", "expert")),
            P(("fsdp", "expert"), None),
            P(("fsdp", "expert")),
            P(("fsdp", "expert")),
            P(("fsdp", "expert")),
            P(("fsdp", "expert"), None),
            P(("fsdp", "expert")),
            P("expert", None, "fsdp"),
            P("expert", "fsdp", None),
        ),
        check_vma=False,
    )
```

profile of v0, /device:TPU:0, one launch (start us, length us, event | category | flops | bytes accessed | tf_op | source)
XLA Modules:
  0.0 1677.8 jit_solution(17687012517512811270)
XLA Ops:
  91.9 196.8 %while.28 = (s32[]{:T(128)}, f32[16,1024]{1,0:T(8,128)S(1)}, f32[16,1024]{1,0:T(8,128)S(1)}, f32[16,1024,64]{1,2,0:T(8,128)}, s32[4]{0:T(128)S(1)}, /*index=5*/s...) while((s32[]{:T(128)}, f32[16,1024]{1,0:T(8,128)S(1)}, ...), condition=%wide.region_5.6_spmd.clone, body=%wide.region_2.5_spmd.clone.sunk | while | flops 2219395072 | bytes 120604920 | solution.py:155
  97.0 13.3 fusion.167
  110.3 13.7 fusion.168
  124.0 16.0 fusion.170
  145.3 13.3 fusion.167
  158.6 13.7 fusion.168
  172.3 17.2 %fusion.170 = f32[16,1024,64]{1,2,0:T(8,128)} fusion(f32[16,1024,64]{1,2,0:T(8,128)} %get-tuple-element.670, f32[16,1024]{1,0:T(8,128)S(1)} %get-tuple-element.634, pred[]{:T(512)S(6)} %compare.12, bf16[512,16,64]{0,2,1:T(8,128)(2,1)} %bitcast.278, f32[16,512,1024]{2,1,0:T(8,128)} %get-tuple-element.632, f32[16,1024]{1,0:T(8,128)S(1)} %select_maximum_fusion.2, ...), kind=kOutput, calls=%fused_computation.18.clone.1 | convolution fusion | flops 1102053376 | bytes 43646976 | tf_op jit(solution)/shard_map/while/body/eval_jaxpr/hqk,khd->hqd/dot_general | solution.py:142
  194.7 13.3 fusion.167
  208.0 13.7 fusion.168
  221.7 17.2 %fusion.170 = f32[16,1024,64]{1,2,0:T(8,128)} fusion(f32[16,1024,64]{1,2,0:T(8,128)} %get-tuple-element.670, f32[16,1024]{1,0:T(8,128)S(1)} %get-tuple-element.634, pred[]{:T(512)S(6)} %compare.12, bf16[512,16,64]{0,2,1:T(8,128)(2,1)} %bitcast.278, f32[16,512,1024]{2,1,0:T(8,128)} %get-tuple-element.632, f32[16,1024]{1,0:T(8,128)S(1)} %select_maximum_fusion.2, ...), kind=kOutput, calls=%fused_computation.18.clone.1 | convolution fusion | flops 1102053376 | bytes 43646976 | tf_op jit(solution)/shard_map/while/body/eval_jaxpr/hqk,khd->hqd/dot_general | solution.py:142
  244.1 13.3 fusion.167
  257.5 13.7 fusion.168
  271.2 17.2 %fusion.170 = f32[16,1024,64]{1,2,0:T(8,128)} fusion(f32[16,1024,64]{1,2,0:T(8,128)} %get-tuple-element.670, f32[16,1024]{1,0:T(8,128)S(1)} %get-tuple-element.634, pred[]{:T(512)S(6)} %compare.12, bf16[512,16,64]{0,2,1:T(8,128)(2,1)} %bitcast.278, f32[16,512,1024]{2,1,0:T(8,128)} %get-tuple-element.632, f32[16,1024]{1,0:T(8,128)S(1)} %select_maximum_fusion.2, ...), kind=kOutput, calls=%fused_computation.18.clone.1 | convolution fusion | flops 1102053376 | bytes 43646976 | tf_op jit(solution)/shard_map/while/body/eval_jaxpr/hqk,khd->hqd/dot_general | solution.py:142
  314.3 101.1 %all_to_all.48 = bf16[16,128,1024]{2,1,0:T(8,128)(2,1)} all-to-all(bf16[16,128,1024]{2,1,0:T(8,128)(2,1)} %bitcast.290), channel_id=1, replica_groups=mesh['fsdp'=2,'expert'=16] {'expert'}, dimensions={0} | all-to-all | bytes 8388608 | tf_op jit(solution)/shard_map/all_to_all | solution.py:184
  415.5 18.4 %all-gather.17.cloned.1.call-done = bf16[1,4096,1024]{2,1,0:T(8,128)(2,1)} async-done(((bf16[1,2048,1024]{2,1,0:T(8,128)(2,1)}), bf16[1,4096,1024]{2,1,0:T(8,128)(2,1)}) %all-gather.17.cloned.1.call-update) | async-done | bytes 8388624 | tf_op jit(solution)/shard_map/all_gather | solution.py:185
  433.9 25.7 %fusion.38 = f32[4096,2048]{1,0:T(8,128)} fusion(bf16[1,4096,1024]{2,1,0:T(8,128)(2,1)} %all-gather.17.cloned.1.call-done, bf16[1,1024,2048]{2,1,0:T(8,128)(2,1)} %param.36), kind=kOutput, calls=%fused_computation.63 | convolution fusion | flops 17179869184 | bytes 46137344 | tf_op jit(solution)/shard_map/erd,edh->erh/dot_general | solution.py:186
  459.6 27.6 %convert_bitcast_fusion.1 = bf16[1,4096,1024]{2,1,0:T(8,128)(2,1)} fusion(bf16[1,2048,1024]{2,1,0:T(8,128)(2,1)S(1)} %copy-done.73, f32[4096,2048]{1,0:T(8,128)} %fusion.38), kind=kOutput, calls=%fused_computation.66 | convolution fusion | flops 17259560960 | bytes 46137344 | tf_op jit(solution)/shard_map/erh,ehd->erd/dot_general | solution.py:188
  487.2 18.1 %reduce-scatter.8.cloned.1.call-done = bf16[1,2048,1024]{2,1,0:T(8,128)(2,1)} async-done(((bf16[1,4096,1024]{2,1,0:T(8,128)(2,1)}), bf16[1,2048,1024]{2,1,0:T(8,128)(2,1)}) %reduce-scatter.8.cloned.1.call-update) | async-done | bytes 4194320 | tf_op jit(solution)/shard_map/reduce_scatter | solution.py:189
  514.6 26.0 %reduce.9 = bf16[2048,1024]{1,0:T(8,128)(2,1)} reduce(bf16[2048,1,1024]{2,1,0:T(2,128)(2,1)} %bitcast.282, bf16[]{:T(256)} %broadcast.411), dimensions={1}, to_apply=%bitcast.212.reduce_sub_computation | reduce | bytes 8388610
  561.9 77.5 %all-to-all-done.1 = bf16[16,2,65536]{2,1,0:T(2,128)(2,1)} async-done(((bf16[16,2,65536]{2,1,0:T(2,128)(2,1)}), bf16[16,2,65536]{2,1,0:T(2,128)(2,1)}, u32[]{:S(2)}, u32[]{:S(2)}) %all-to-all-start.1) | async-done | bytes 4194336 | tf_op jit(solution)/shard_map/all_to_all | solution.py:192
  658.8 20.9 %gather_fusion = bf16[1024,1024]{1,0:T(8,128)(2,1)} fusion(bf16[16,128,1024]{2,1,0:T(8,128)(2,1)} %bitcast.279, s32[1024]{0:T(1024)S(1)} %bitcast.275), kind=kCustom, calls=%fused_computation | custom fusion | bytes 4202496 | tf_op jit(solution)/shard_map/gather | solution.py:182
  698.6 113.6 %all_to_all.49 = bf16[16,128,1024]{2,1,0:T(8,128)(2,1)} all-to-all(bf16[16,128,1024]{2,1,0:T(8,128)(2,1)} %bitcast.289), channel_id=1, replica_groups=mesh['fsdp'=2,'expert'=16] {'expert'}, dimensions={0} | all-to-all | bytes 8388608 | tf_op jit(solution)/shard_map/all_to_all | solution.py:199
  812.3 18.4 %all-gather.19.cloned.1.call-done = bf16[1,4096,1024]{2,1,0:T(8,128)(2,1)} async-done(((bf16[1,2048,1024]{2,1,0:T(8,128)(2,1)}), bf16[1,4096,1024]{2,1,0:T(8,128)(2,1)}) %all-gather.19.cloned.1.call-update) | async-done | bytes 8388624 | tf_op jit(solution)/shard_map/all_gather | solution.py:203
  830.7 42.2 %fusion.31 = bf16[4096,2048]{1,0:T(8,128)(2,1)} fusion(f32[4096,2048]{1,0:T(8,128)} %fusion.38, bf16[1,4096,1024]{2,1,0:T(8,128)(2,1)} %all-gather.19.cloned.1.call-done, bf16[1,2048,1024]{2,1,0:T(8,128)(2,1)} %param.37), kind=kOutput, calls=%fused_computation.52 | convolution fusion | flops 17347641344 | bytes 62914560 | tf_op jit(solution)/shard_map/erd,ehd->erh/dot_general | solution.py:204
  872.9 23.9 %convert_bitcast_fusion = bf16[1,4096,1024]{2,1,0:T(8,128)(2,1)} fusion(bf16[4096,2048]{1,0:T(8,128)(2,1)} %fusion.31, bf16[1,1024,2048]{2,1,0:T(8,128)(2,1)} %param.36), kind=kOutput, calls=%fused_computation.65 | convolution fusion | flops 17184063488 | bytes 29360128 | tf_op jit(solution)/shard_map/erh,edh->erd/dot_general | solution.py:210
  896.9 18.1 %reduce-scatter.10.cloned.1.call-done = bf16[1,2048,1024]{2,1,0:T(8,128)(2,1)} async-done(((bf16[1,4096,1024]{2,1,0:T(8,128)(2,1)}), bf16[1,2048,1024]{2,1,0:T(8,128)(2,1)}) %reduce-scatter.10.cloned.1.call-update) | async-done | bytes 4194320 | tf_op jit(solution)/shard_map/reduce_scatter | solution.py:211
  923.6 26.0 %reduce.10 = bf16[2048,1024]{1,0:T(8,128)(2,1)} reduce(bf16[2048,1,1024]{2,1,0:T(2,128)(2,1)} %bitcast.283, bf16[]{:T(256)} %broadcast.411), dimensions={1}, to_apply=%bitcast.211.reduce_sub_computation | reduce | bytes 8388610
  971.7 78.2 %all-to-all-done.3 = bf16[16,2,65536]{2,1,0:T(2,128)(2,1)} async-done(((bf16[16,2,65536]{2,1,0:T(2,128)(2,1)}), bf16[16,2,65536]{2,1,0:T(2,128)(2,1)}, u32[]{:S(2)}, u32[]{:S(2)}) %all-to-all-start.3) | async-done | bytes 4194336 | tf_op jit(solution)/shard_map/all_to_all | solution.py:215
  1049.9 12.4 reshape.461
  1069.5 15.5 gather_fusion.1
  1108.8 351.3 %while.29 = (s32[]{:T(128)}, f32[1024,16,64]{0,2,1:T(8,128)}, f32[4,512,2048]{2,1,0:T(8,128)}, s32[4]{0:T(128)S(1)}, bf16[2048,2048]{0,1:T(8,128)(2,1)}, /*index...) while((s32[]{:T(128)}, f32[1024,16,64]{0,2,1:T(8,128)}, ...), condition=%wide.region_23.24_spmd.clone, body=%wide.region_22.23_spmd.clone.sunk | while | flops 5440538624 | bytes 305875520 | solution.py:256
  1115.7 13.2 fusion.182
  1128.8 15.5 fusion.184
  1144.4 20.7 %fusion.183 = bf16[16,1024,512]{1,2,0:T(8,128)(2,1)} fusion(f32[16,512,1024]{2,1,0:T(8,128)} %fusion.182, f32[16,1024]{1,0:T(8,128)S(1)} %get-tuple-element.741, f32[16,1024]{1,0:T(8,128)S(1)} %get-tuple-element.739, pred[1024,512]{0,1:T(8,128)(4,1)S(1)} %copy-done.21, bf16[512,16,64]{0,2,1:T(8,128)(2,1)S(1)} %bitcast.286, ...), kind=kOutput, calls=%fused_computation.30.clone.1 | convolution fusion | flops 1115684864 | bytes 54132736 | tf_op jit(solution)/shard_map/while/body/eval_jaxpr/qhd,khd->hqk/dot_general | solution.py:238
  1201.7 13.2 fusion.182
  1214.9 15.6 fusion.184
  1230.5 20.8 %fusion.183 = bf16[16,1024,512]{1,2,0:T(8,128)(2,1)} fusion(f32[16,512,1024]{2,1,0:T(8,128)} %fusion.182, f32[16,1024]{1,0:T(8,128)S(1)} %get-tuple-element.741, f32[16,1024]{1,0:T(8,128)S(1)} %get-tuple-element.739, pred[1024,512]{0,1:T(8,128)(4,1)S(1)} %copy-done.21, bf16[512,16,64]{0,2,1:T(8,128)(2,1)S(1)} %bitcast.286, ...), kind=kOutput, calls=%fused_computation.30.clone.1 | convolution fusion | flops 1115684864 | bytes 54132736 | tf_op jit(solution)/shard_map/while/body/eval_jaxpr/qhd,khd->hqk/dot_general | solution.py:238
  1290.2 13.2 fusion.182
  1303.4 15.4 fusion.184
  1318.9 20.7 %fusion.183 = bf16[16,1024,512]{1,2,0:T(8,128)(2,1)} fusion(f32[16,512,1024]{2,1,0:T(8,128)} %fusion.182, f32[16,1024]{1,0:T(8,128)S(1)} %get-tuple-element.741, f32[16,1024]{1,0:T(8,128)S(1)} %get-tuple-element.739, pred[1024,512]{0,1:T(8,128)(4,1)S(1)} %copy-done.21, bf16[512,16,64]{0,2,1:T(8,128)(2,1)S(1)} %bitcast.286, ...), kind=kOutput, calls=%fused_computation.30.clone.1 | convolution fusion | flops 1115684864 | bytes 54132736 | tf_op jit(solution)/shard_map/while/body/eval_jaxpr/qhd,khd->hqk/dot_general | solution.py:238
  1378.3 13.1 fusion.182
  1391.4 15.4 fusion.184
  1406.9 20.7 %fusion.183 = bf16[16,1024,512]{1,2,0:T(8,128)(2,1)} fusion(f32[16,512,1024]{2,1,0:T(8,128)} %fusion.182, f32[16,1024]{1,0:T(8,128)S(1)} %get-tuple-element.741, f32[16,1024]{1,0:T(8,128)S(1)} %get-tuple-element.739, pred[1024,512]{0,1:T(8,128)(4,1)S(1)} %copy-done.21, bf16[512,16,64]{0,2,1:T(8,128)(2,1)S(1)} %bitcast.286, ...), kind=kOutput, calls=%fused_computation.30.clone.1 | convolution fusion | flops 1115684864 | bytes 54132736 | tf_op jit(solution)/shard_map/while/body/eval_jaxpr/qhd,khd->hqk/dot_general | solution.py:238
  1500.2 24.1 %fusion.51 = f32[1,1024,2048]{2,1,0:T(8,128)} fusion(bf16[4096,2048]{1,0:T(8,128)(2,1)} %fusion.31, bf16[1,4096,1024]{2,1,0:T(8,128)(2,1)} %all-gather.17.cloned.1.call-done), kind=kOutput, calls=%fused_computation.84 | convolution fusion | flops 17179869184 | bytes 33554432 | tf_op jit(solution)/shard_map/erd,erh->edh/dot_general | solution.py:209
  1524.3 26.8 %fusion.54 = f32[1,2048,1024]{2,1,0:T(8,128)} fusion(bf16[1,4096,1024]{2,1,0:T(8,128)(2,1)} %all-gather.19.cloned.1.call-done, f32[4096,2048]{1,0:T(8,128)} %fusion.38), kind=kOutput, calls=%fused_computation.85 | convolution fusion | flops 17255366656 | bytes 50331648 | tf_op jit(solution)/shard_map/erh,erd->ehd/dot_general | solution.py:205
  1555.3 12.6 fusion.111
  1578.7 59.0 %all-reduce.8 = (f32[1024]{0:T(1024)S(1)}, f32[1024]{0:T(1024)S(1)}, f32[1024]{0:T(1024)S(1)}, f32[1024]{0:T(1024)S(1)}, f32[1024]{0:T(1024)S(1)}, /*index=5*/f3...) all-reduce(f32[1024]{0:T(1024)S(1)} %get-tuple-element.402, ...), channel_id=4, replica_groups=mesh['fsdp'=2,'expert'=16] {'fsdp','expert'}, use_global_device_ids=true, to_apply=%region_27.28.clone | all-reduce | flops 8192 | bytes 65536
  1652.6 18.4 %reduce-scatter.12.cloned.1.call-done = f32[32,3072]{1,0:T(8,128)} async-done(((f32[1024,3072]{1,0:T(8,128)}), f32[32,3072]{1,0:T(8,128)}) %reduce-scatter.12.cloned.1.call-update) | async-done | bytes 393232 | tf_op jit(solution)/shard_map/reduce_scatter | solution.py:280
  (437 shorter events, 478.3 us)
Async XLA Ops:
  7.2 21.9 %all-gather.13.cloned.1.call-start = ((), (), s32[]{:S(2)}) async-start(), calls=%async_computation.9 | async-start | bytes 9437184 | tf_op jit(solution)/shard_map/all_gather | solution.py:74
  7.9 285.7 %all-gather.15.cloned.1.call-start = ((), (), s32[]{:S(2)}) async-start(), calls=%async_computation.10 | async-start | bytes 3145728 | tf_op jit(solution)/shard_map/all_gather | solution.py:77
  10.6 18.5 %copy-start.49 = (f32[2,1,512]{2,1,0:T(1,128)}, f32[2,1,512]{2,1,0:T(1,128)S(1)}, u32[]{:S(2)}) copy-start(f32[2,1,512]{2,1,0:T(1,128)S(1)} %convert_element_type.200) | copy-start | bytes 12292
  13.0 16.0 copy-start.62
  21.0 17.3 %copy-start.7 = (bf16[1,1024,1024]{1,2,0:T(8,128)(2,1)}, bf16[1,1024,1024]{1,2,0:T(8,128)(2,1)S(1)}, u32[]{:S(2)}) copy-start(bf16[1,1024,1024]{1,2,0:T(8,128)(2,1)S(1)} %copy.127) | copy-start | bytes 6291460
  21.4 16.9 %copy-start.38 = (f32[1024]{0:T(1024)}, f32[1024]{0:T(1024)S(1)}, u32[]{:S(2)}) copy-start(f32[1024]{0:T(1024)S(1)} %broadcast_multiply_fusion.5) | copy-start | bytes 12292
  22.0 16.3 copy-start.51
  41.4 12.2 copy-start.68
  41.4 14.6 copy-start.69
  41.4 17.0 %copy-start.42 = (s32[1,1024,1]{1,2,0:T(1,128)S(1)}, s32[1,1024,1]{1,2,0:T(1,128)}, u32[]{:S(2)}) copy-start(s32[1,1024,1]{1,2,0:T(1,128)} %param.23) | copy-start | bytes 12292
  41.4 21.8 %copy-start.61 = (bf16[512,16]{0,1:T(8,128)(2,1)S(1)}, bf16[512,16]{0,1:T(8,128)(2,1)}, u32[]{:S(2)}) copy-start(bf16[512,16]{0,1:T(8,128)(2,1)} %param.34) | copy-start | bytes 49156
  44.1 24.8 %collective-permute-start = (bf16[1024,2048]{1,0:T(8,128)(2,1)}, bf16[1024,2048]{1,0:T(8,128)(2,1)}, u32[]{:S(2)}, u32[]{:S(2)}) collective-permute-start(bf16[1024,2048]{1,0:T(8,128)(2,1)} %pad_maximum_fusion.1), channel_id=1, source_target_pairs={{0,16},{1,17},{2,18},{3,19},{4,20},{5,21},{6,22},{7,23},{8,24},{9,... | collective-permute-start | bytes 12582920 | tf_op jit(solution)/shard_map/ppermute | solution.py:16
  48.2 385.6 %all-gather.17.cloned.1.call-start = ((), (), s32[]{:S(2)}) async-start(), calls=%async_computation.11 | async-start | bytes 12582912 | tf_op jit(solution)/shard_map/all_gather | solution.py:185
  288.6 10.5 copy-start.1
  288.6 10.5 copy-start.23
  304.8 110.6 %copy-start.40 = (f32[1024]{0:T(1024)}, f32[1024]{0:T(1024)S(1)}, u32[]{:S(2)}) copy-start(f32[1024]{0:T(1024)S(1)} %get-tuple-element.487) | copy-start | bytes 12292
  304.9 110.6 %copy-start.57 = (f32[1024]{0:T(1024)}, f32[1024]{0:T(1024)S(1)}, u32[]{:S(2)}) copy-start(f32[1024]{0:T(1024)S(1)} %fusion.94) | copy-start | bytes 12292
  415.5 89.9 %reduce-scatter.8.cloned.1.call-start = ((), (), s32[]{:S(2)}) async-start(), calls=%async_computation.12 | async-start | bytes 12582912 | tf_op jit(solution)/shard_map/reduce_scatter | solution.py:189
  433.9 25.7 %copy-start.73 = (bf16[1,2048,1024]{2,1,0:T(8,128)(2,1)S(1)}, bf16[1,2048,1024]{2,1,0:T(8,128)(2,1)}, u32[]{:S(2)}) copy-start(bf16[1,2048,1024]{2,1,0:T(8,128)(2,1)} %param.37) | copy-start | bytes 12582916
  552.0 87.4 %all-to-all-start.1 = ((bf16[16,2,65536]{2,1,0:T(2,128)(2,1)}), bf16[16,2,65536]{2,1,0:T(2,128)(2,1)}, u32[]{:S(2)}, u32[]{:S(2)}) async-start(bf16[16,2,65536]{2,1,0:T(2,128)(2,1)} %reshape.458), calls=%async_computation.2 | async-start | bytes 8388608 | tf_op jit(solution)/shard_map/all_to_all | solution.py:192
  559.0 271.8 %all-gather.19.cloned.1.call-start = ((), (), s32[]{:S(2)}) async-start(), calls=%async_computation.13 | async-start | bytes 12582912 | tf_op jit(solution)/shard_map/all_gather | solution.py:203
  561.9 121.7 %copy-start.12 = (bf16[1,1024,1024]{1,2,0:T(8,128)(2,1)}, bf16[1,1024,1024]{1,2,0:T(8,128)(2,1)S(1)}, u32[]{:S(2)}) copy-start(bf16[1,1024,1024]{1,2,0:T(8,128)(2,1)S(1)} %copy.135) | copy-start | bytes 6291460
  812.3 102.7 %reduce-scatter.10.cloned.1.call-start = ((), (), s32[]{:S(2)}) async-start(), calls=%async_computation.14 | async-start | bytes 12582912 | tf_op jit(solution)/shard_map/reduce_scatter | solution.py:211
  961.1 88.9 %all-to-all-start.3 = ((bf16[16,2,65536]{2,1,0:T(2,128)(2,1)}), bf16[16,2,65536]{2,1,0:T(2,128)(2,1)}, u32[]{:S(2)}, u32[]{:S(2)}) async-start(bf16[16,2,65536]{2,1,0:T(2,128)(2,1)} %reshape.460), calls=%async_computation.5 | async-start | bytes 8388608 | tf_op jit(solution)/shard_map/all_to_all | solution.py:215
  968.1 530.7 %reduce-scatter.16.cloned.1.call-start = ((), (), s32[]{:S(2)}) async-start(), calls=%async_computation.17 | async-start | bytes 540672
  971.6 681.0 %reduce-scatter.14.cloned.1.call-start = ((), (), s32[]{:S(2)}) async-start(), calls=%async_computation.16 | async-start | bytes 4325376 | tf_op jit(solution)/shard_map/reduce_scatter | solution.py:285
  1107.3 563.7 %reduce-scatter.12.cloned.1.call-start = ((), (), s32[]{:S(2)}) async-start(), calls=%async_computation.15 | async-start | bytes 12976128 | tf_op jit(solution)/shard_map/reduce_scatter | solution.py:280
  1109.0 35.3 %copy-start.36 = (f32[16,1024]{1,0:T(8,128)}, f32[16,1024]{1,0:T(8,128)S(1)}, u32[]{:S(2)}) copy-start(f32[16,1024]{1,0:T(8,128)S(1)} %get-tuple-element.741) | copy-start | bytes 196612 | tf_op jit(solution)/shard_map/while
  1109.0 35.3 %copy-start.45 = (f32[16,1024]{1,0:T(8,128)}, f32[16,1024]{1,0:T(8,128)S(1)}, u32[]{:S(2)}) copy-start(f32[16,1024]{1,0:T(8,128)S(1)} %get-tuple-element.739) | copy-start | bytes 196612 | tf_op jit(solution)/shard_map/while
  1128.8 15.5 copy-start.16
  1128.8 15.5 copy-start.21
  1165.1 12.0 copy-start
  1195.0 35.4 %copy-start.36 = (f32[16,1024]{1,0:T(8,128)}, f32[16,1024]{1,0:T(8,128)S(1)}, u32[]{:S(2)}) copy-start(f32[16,1024]{1,0:T(8,128)S(1)} %get-tuple-element.741) | copy-start | bytes 196612 | tf_op jit(solution)/shard_map/while
  1195.0 35.4 %copy-start.45 = (f32[16,1024]{1,0:T(8,128)}, f32[16,1024]{1,0:T(8,128)S(1)}, u32[]{:S(2)}) copy-start(f32[16,1024]{1,0:T(8,128)S(1)} %get-tuple-element.739) | copy-start | bytes 196612 | tf_op jit(solution)/shard_map/while
  1214.9 15.6 copy-start.16
  1214.9 15.6 copy-start.21
  1251.2 12.0 copy-start
  1283.5 35.3 %copy-start.36 = (f32[16,1024]{1,0:T(8,128)}, f32[16,1024]{1,0:T(8,128)S(1)}, u32[]{:S(2)}) copy-start(f32[16,1024]{1,0:T(8,128)S(1)} %get-tuple-element.741) | copy-start | bytes 196612 | tf_op jit(solution)/shard_map/while
  1283.5 35.3 %copy-start.45 = (f32[16,1024]{1,0:T(8,128)}, f32[16,1024]{1,0:T(8,128)S(1)}, u32[]{:S(2)}) copy-start(f32[16,1024]{1,0:T(8,128)S(1)} %get-tuple-element.739) | copy-start | bytes 196612 | tf_op jit(solution)/shard_map/while
  1303.4 15.5 copy-start.16
  1303.4 15.5 copy-start.21
  1339.6 11.9 copy-start
  1371.7 35.2 %copy-start.36 = (f32[16,1024]{1,0:T(8,128)}, f32[16,1024]{1,0:T(8,128)S(1)}, u32[]{:S(2)}) copy-start(f32[16,1024]{1,0:T(8,128)S(1)} %get-tuple-element.741) | copy-start | bytes 196612 | tf_op jit(solution)/shard_map/while
  1371.7 35.2 %copy-start.45 = (f32[16,1024]{1,0:T(8,128)}, f32[16,1024]{1,0:T(8,128)S(1)}, u32[]{:S(2)}) copy-start(f32[16,1024]{1,0:T(8,128)S(1)} %get-tuple-element.739) | copy-start | bytes 196612 | tf_op jit(solution)/shard_map/while
  1391.4 15.5 copy-start.16
  1391.4 15.5 copy-start.21
  1427.6 11.9 copy-start
  1466.2 12.5 collective-permute-start.1
  (70 other events, 375.9 us)
Sparse Core Ops, SparseCore 0:
  9.6 19.4 all-gather.12
  48.4 11.8 all-gather.14
  415.6 18.2 all-gather.16
  487.3 17.9 reduce-scatter.7
  812.4 18.2 all-gather.18
  897.0 17.9 reduce-scatter.9
  971.8 180.1 reduce-scatter.15
  1154.9 147.8 reduce-scatter.13
  1497.0 173.9 reduce-scatter.11
where the time goes:
time: 1690 us; the launch traced here: 1680 us
  matrix products  609 us (36%)
  blocking collectives  293 us (17%)
  local copies, waits for them, and re-layouts  287 us (17%)
  waiting for transfers between devices  255 us (15%)
  other arithmetic  192 us (11%)
  starting transfers between devices  20.1 us (1%)
    unnamed x161, local copies, waits for them, and re-layouts  122 us
    all_to_all x1, blocking collectives, body(): lax.all_to_all(dispatch(d_expert_value), 'expert', split_axis=0, concat_a...  114 us
    all_to_all x1, blocking collectives, body(): lax.all_to_all(dispatch(mixed_low), 'expert', split_axis=0, concat_axis=1...  101 us
    dot_general x4, matrix products, backward_block(): jnp.einsum('qhd,khd->hqk', d_context_heads, value_heads, preferred_elemen...  82.9 us
    all_to_all x1, waiting for transfers between devices, body(): lax.all_to_all(d_rows, 'expert', split_axis=1, concat_axis=0, tiled=True)  78.2 us
    all_to_all x1, waiting for transfers between devices, body(): lax.all_to_all(expert_rows, 'expert', split_axis=1, concat_axis=0, tiled=...  77.5 us
    dot_general x4, matrix products, forward_block(): jnp.einsum('hqk,khd->hqd', weights.astype(jnp.bfloat16), value_heads, pre...  67.7 us
    dot_general x4, matrix products, backward_block(): jnp.einsum('hqk,qhd->khd', probs_part.astype(jnp.bfloat16), d_context_hea...  62 us
  transfers between devices with their start and end apart: 13, of which 8 were waited for; matrix products, arithmetic and copies ran while one was open for 46% of the time, Pallas kernels for 0%

commit v1 on v0

--- a/solution.py
+++ b/solution.py
@@ -196,8 +196,14 @@
     d_expert_bias = jnp.sum(out_cot, axis=0)
     d_gate = jnp.sum(out_cot * expert_value, axis=-1)
     d_expert_value = (gate_value[:, None] * out_cot).astype(jnp.bfloat16)
-    grads_arrived = lax.all_to_all(
-        dispatch(d_expert_value), "expert", split_axis=0, concat_axis=1, tiled=True
+    grads_arrived = jnp.concatenate(
+        lax.all_to_all(
+            jnp.stack(jnp.split(dispatch(d_expert_value), lax.axis_size("expert"), axis=0)),
+            "expert",
+            0,
+            0,
+        ),
+        axis=1,
     )
     unused_out, gelu_back = jax.vjp(partial(jax.nn.gelu, approximate=True), pre_act)
     grad_in = lax.all_gather(grads_arrived, "fsdp", axis=1, tiled=True)

time: 1690 us -> 1700 us (level)
    unnamed x161 -> x176, local copies, waits for them, and re-layouts: 122 us -> 137 us
  transfers between devices with their start and end apart: 13 -> 13, of which waited for: 8 -> 8; matrix products, arithmetic and copies ran while one was open for 46% -> 45% of each run, Pallas kernels for 0% -> 0%
where the time goes in v1:
time: 1700 us; the launch traced here: 1690 us
  matrix products  609 us (36%)
  local copies, waits for them, and re-layouts  302 us (18%)
  blocking collectives  293 us (17%)
  waiting for transfers between devices  255 us (15%)
  other arithmetic  192 us (11%)
  starting transfers between devices  20.1 us (1%)
    unnamed x176, local copies, waits for them, and re-layouts  137 us
    all_to_all x1, blocking collectives, body(): lax.all_to_all(jnp.stack(jnp.split(dispatch(d_expert_value), lax.axis_siz...  113 us
    all_to_all x1, blocking collectives, body(): lax.all_to_all(dispatch(mixed_low), 'expert', split_axis=0, concat_axis=1...  101 us
    dot_general x4, matrix products, backward_block(): jnp.einsum('qhd,khd->hqk', d_context_heads, value_heads, preferred_elemen...  82.9 us
    all_to_all x1, waiting for transfers between devices, body(): lax.all_to_all(d_rows, 'expert', split_axis=1, concat_axis=0, tiled=True)  78.3 us
    all_to_all x1, waiting for transfers between devices, body(): lax.all_to_all(expert_rows, 'expert', split_axis=1, concat_axis=0, tiled=...  77.5 us
    dot_general x4, matrix products, forward_block(): jnp.einsum('hqk,khd->hqd', weights.astype(jnp.bfloat16), value_heads, pre...  67.7 us
    dot_general x4, matrix products, backward_block(): jnp.einsum('hqk,qhd->khd', probs_part.astype(jnp.bfloat16), d_context_hea...  62 us
  transfers between devices with their start and end apart: 13, of which 8 were waited for; matrix products, arithmetic and copies ran while one was open for 45% of the time, Pallas kernels for 0%

profile of v1, /device:TPU:0, one launch (start us, length us, event | category | flops | bytes accessed | tf_op | source)
XLA Modules:
  0.0 1693.2 jit_solution(4760277834244362283)
XLA Ops:
  91.9 196.8 %while.28 = (s32[]{:T(128)}, f32[16,1024]{1,0:T(8,128)S(1)}, f32[16,1024]{1,0:T(8,128)S(1)}, f32[16,1024,64]{1,2,0:T(8,128)}, s32[4]{0:T(128)S(1)}, /*index=5*/s...) while((s32[]{:T(128)}, f32[16,1024]{1,0:T(8,128)S(1)}, ...), condition=%wide.region_5.6_spmd.clone, body=%wide.region_2.5_spmd.clone.sunk | while | flops 2219395072 | bytes 120604920 | solution.py:155
  97.0 13.3 fusion.183
  110.3 13.7 fusion.184
  124.0 16.0 fusion.186
  145.3 13.3 fusion.183
  158.6 13.7 fusion.184
  172.3 17.2 %fusion.186 = f32[16,1024,64]{1,2,0:T(8,128)} fusion(f32[16,1024,64]{1,2,0:T(8,128)} %get-tuple-element.670, f32[16,1024]{1,0:T(8,128)S(1)} %get-tuple-element.634, pred[]{:T(512)S(6)} %compare.12, bf16[512,16,64]{0,2,1:T(8,128)(2,1)} %bitcast.341, f32[16,512,1024]{2,1,0:T(8,128)} %get-tuple-element.632, f32[16,1024]{1,0:T(8,128)S(1)} %select_maximum_fusion.2, ...), kind=kOutput, calls=%fused_computation.18.clone.1 | convolution fusion | flops 1102053376 | bytes 43646976 | tf_op jit(solution)/shard_map/while/body/eval_jaxpr/hqk,khd->hqd/dot_general | solution.py:142
  194.7 13.3 fusion.183
  208.0 13.7 fusion.184
  221.7 17.2 %fusion.186 = f32[16,1024,64]{1,2,0:T(8,128)} fusion(f32[16,1024,64]{1,2,0:T(8,128)} %get-tuple-element.670, f32[16,1024]{1,0:T(8,128)S(1)} %get-tuple-element.634, pred[]{:T(512)S(6)} %compare.12, bf16[512,16,64]{0,2,1:T(8,128)(2,1)} %bitcast.341, f32[16,512,1024]{2,1,0:T(8,128)} %get-tuple-element.632, f32[16,1024]{1,0:T(8,128)S(1)} %select_maximum_fusion.2, ...), kind=kOutput, calls=%fused_computation.18.clone.1 | convolution fusion | flops 1102053376 | bytes 43646976 | tf_op jit(solution)/shard_map/while/body/eval_jaxpr/hqk,khd->hqd/dot_general | solution.py:142
  244.1 13.3 fusion.183
  257.5 13.7 fusion.184
  271.2 17.2 %fusion.186 = f32[16,1024,64]{1,2,0:T(8,128)} fusion(f32[16,1024,64]{1,2,0:T(8,128)} %get-tuple-element.670, f32[16,1024]{1,0:T(8,128)S(1)} %get-tuple-element.634, pred[]{:T(512)S(6)} %compare.12, bf16[512,16,64]{0,2,1:T(8,128)(2,1)} %bitcast.341, f32[16,512,1024]{2,1,0:T(8,128)} %get-tuple-element.632, f32[16,1024]{1,0:T(8,128)S(1)} %select_maximum_fusion.2, ...), kind=kOutput, calls=%fused_computation.18.clone.1 | convolution fusion | flops 1102053376 | bytes 43646976 | tf_op jit(solution)/shard_map/while/body/eval_jaxpr/hqk,khd->hqd/dot_general | solution.py:142
  314.3 101.1 %all_to_all.41 = bf16[16,128,1024]{2,1,0:T(8,128)(2,1)} all-to-all(bf16[16,128,1024]{2,1,0:T(8,128)(2,1)} %bitcast.352), channel_id=1, replica_groups=mesh['fsdp'=2,'expert'=16] {'expert'}, dimensions={0} | all-to-all | bytes 8388608 | tf_op jit(solution)/shard_map/all_to_all | solution.py:184
  415.5 18.4 %all-gather.17.cloned.1.call-done = bf16[1,4096,1024]{2,1,0:T(8,128)(2,1)} async-done(((bf16[1,2048,1024]{2,1,0:T(8,128)(2,1)}), bf16[1,4096,1024]{2,1,0:T(8,128)(2,1)}) %all-gather.17.cloned.1.call-update) | async-done | bytes 8388624 | tf_op jit(solution)/shard_map/all_gather | solution.py:185
  433.9 25.7 %fusion.38 = f32[4096,2048]{1,0:T(8,128)} fusion(bf16[1,4096,1024]{2,1,0:T(8,128)(2,1)} %all-gather.17.cloned.1.call-done, bf16[1,1024,2048]{2,1,0:T(8,128)(2,1)} %param.36), kind=kOutput, calls=%fused_computation.63 | convolution fusion | flops 17179869184 | bytes 46137344 | tf_op jit(solution)/shard_map/erd,edh->erh/dot_general | solution.py:186
  459.6 27.6 %convert_bitcast_fusion.1 = bf16[1,4096,1024]{2,1,0:T(8,128)(2,1)} fusion(bf16[1,2048,1024]{2,1,0:T(8,128)(2,1)S(1)} %copy-done.73, f32[4096,2048]{1,0:T(8,128)} %fusion.38), kind=kOutput, calls=%fused_computation.66 | convolution fusion | flops 17259560960 | bytes 46137344 | tf_op jit(solution)/shard_map/erh,ehd->erd/dot_general | solution.py:188
  487.2 18.1 %reduce-scatter.8.cloned.1.call-done = bf16[1,2048,1024]{2,1,0:T(8,128)(2,1)} async-done(((bf16[1,4096,1024]{2,1,0:T(8,128)(2,1)}), bf16[1,2048,1024]{2,1,0:T(8,128)(2,1)}) %reduce-scatter.8.cloned.1.call-update) | async-done | bytes 4194320 | tf_op jit(solution)/shard_map/reduce_scatter | solution.py:189
  514.6 26.0 %reduce.9 = bf16[2048,1024]{1,0:T(8,128)(2,1)} reduce(bf16[2048,1,1024]{2,1,0:T(2,128)(2,1)} %bitcast.345, bf16[]{:T(256)} %broadcast.411), dimensions={1}, to_apply=%bitcast.275.reduce_sub_computation | reduce | bytes 8388610
  561.9 77.5 %all-to-all-done.1 = bf16[16,2,65536]{2,1,0:T(2,128)(2,1)} async-done(((bf16[16,2,65536]{2,1,0:T(2,128)(2,1)}), bf16[16,2,65536]{2,1,0:T(2,128)(2,1)}, u32[]{:S(2)}, u32[]{:S(2)}) %all-to-all-start.1) | async-done | bytes 4194336 | tf_op jit(solution)/shard_map/all_to_all | solution.py:192
  658.8 20.9 %gather_fusion = bf16[1024,1024]{1,0:T(8,128)(2,1)} fusion(bf16[16,128,1024]{2,1,0:T(8,128)(2,1)} %bitcast.342, s32[1024]{0:T(1024)S(1)} %bitcast.338), kind=kCustom, calls=%fused_computation | custom fusion | bytes 4202496 | tf_op jit(solution)/shard_map/gather | solution.py:182
  714.2 113.4 %all_to_all.42 = bf16[16,1,128,1024]{3,2,1,0:T(8,128)(2,1)} all-to-all(bf16[16,1,128,1024]{3,2,1,0:T(8,128)(2,1)S(1)} %fusion.88), channel_id=1, replica_groups=mesh['fsdp'=2,'expert'=16] {'expert'}, dimensions={0} | all-to-all | bytes 8388608 | tf_op jit(solution)/shard_map/all_to_all | solution.py:200
  827.7 18.4 %all-gather.19.cloned.1.call-done = bf16[1,4096,1024]{2,1,0:T(8,128)(2,1)} async-done(((bf16[1,2048,1024]{2,1,0:T(8,128)(2,1)}), bf16[1,4096,1024]{2,1,0:T(8,128)(2,1)}) %all-gather.19.cloned.1.call-update) | async-done | bytes 8388624 | tf_op jit(solution)/shard_map/all_gather | solution.py:209
  846.1 42.2 %fusion.31 = bf16[4096,2048]{1,0:T(8,128)(2,1)} fusion(f32[4096,2048]{1,0:T(8,128)} %fusion.38, bf16[1,4096,1024]{2,1,0:T(8,128)(2,1)} %all-gather.19.cloned.1.call-done, bf16[1,2048,1024]{2,1,0:T(8,128)(2,1)} %param.37), kind=kOutput, calls=%fused_computation.52 | convolution fusion | flops 17347641344 | bytes 62914560 | tf_op jit(solution)/shard_map/erd,ehd->erh/dot_general | solution.py:210
  888.3 23.9 %convert_bitcast_fusion = bf16[1,4096,1024]{2,1,0:T(8,128)(2,1)} fusion(bf16[4096,2048]{1,0:T(8,128)(2,1)} %fusion.31, bf16[1,1024,2048]{2,1,0:T(8,128)(2,1)} %param.36), kind=kOutput, calls=%fused_computation.65 | convolution fusion | flops 17184063488 | bytes 29360128 | tf_op jit(solution)/shard_map/erh,edh->erd/dot_general | solution.py:216
  912.2 18.1 %reduce-scatter.10.cloned.1.call-done = bf16[1,2048,1024]{2,1,0:T(8,128)(2,1)} async-done(((bf16[1,4096,1024]{2,1,0:T(8,128)(2,1)}), bf16[1,2048,1024]{2,1,0:T(8,128)(2,1)}) %reduce-scatter.10.cloned.1.call-update) | async-done | bytes 4194320 | tf_op jit(solution)/shard_map/reduce_scatter | solution.py:217
  939.0 26.0 %reduce.10 = bf16[2048,1024]{1,0:T(8,128)(2,1)} reduce(bf16[2048,1,1024]{2,1,0:T(2,128)(2,1)} %bitcast.346, bf16[]{:T(256)} %broadcast.411), dimensions={1}, to_apply=%bitcast.274.reduce_sub_computation | reduce | bytes 8388610
  987.1 78.3 %all-to-all-done.3 = bf16[16,2,65536]{2,1,0:T(2,128)(2,1)} async-done(((bf16[16,2,65536]{2,1,0:T(2,128)(2,1)}), bf16[16,2,65536]{2,1,0:T(2,128)(2,1)}, u32[]{:S(2)}, u32[]{:S(2)}) %all-to-all-start.3) | async-done | bytes 4194336 | tf_op jit(solution)/shard_map/all_to_all | solution.py:221
  1065.3 12.4 reshape.494
  1084.9 15.5 gather_fusion.1
  1124.2 351.3 %while.29 = (s32[]{:T(128)}, f32[1024,16,64]{0,2,1:T(8,128)}, f32[4,512,2048]{2,1,0:T(8,128)}, s32[4]{0:T(128)S(1)}, bf16[2048,2048]{0,1:T(8,128)(2,1)}, /*index...) while((s32[]{:T(128)}, f32[1024,16,64]{0,2,1:T(8,128)}, ...), condition=%wide.region_23.24_spmd.clone, body=%wide.region_22.23_spmd.clone.sunk | while | flops 5440538624 | bytes 305875520 | solution.py:262
  1131.1 13.2 fusion.198
  1144.3 15.5 fusion.200
  1159.8 20.7 %fusion.199 = bf16[16,1024,512]{1,2,0:T(8,128)(2,1)} fusion(f32[16,512,1024]{2,1,0:T(8,128)} %fusion.198, f32[16,1024]{1,0:T(8,128)S(1)} %get-tuple-element.741, f32[16,1024]{1,0:T(8,128)S(1)} %get-tuple-element.739, pred[1024,512]{0,1:T(8,128)(4,1)S(1)} %copy-done.21, bf16[512,16,64]{0,2,1:T(8,128)(2,1)S(1)} %bitcast.349, ...), kind=kOutput, calls=%fused_computation.30.clone.1 | convolution fusion | flops 1115684864 | bytes 54132736 | tf_op jit(solution)/shard_map/while/body/eval_jaxpr/qhd,khd->hqk/dot_general | solution.py:244
  1217.1 13.2 fusion.198
  1230.3 15.6 fusion.200
  1245.9 20.8 %fusion.199 = bf16[16,1024,512]{1,2,0:T(8,128)(2,1)} fusion(f32[16,512,1024]{2,1,0:T(8,128)} %fusion.198, f32[16,1024]{1,0:T(8,128)S(1)} %get-tuple-element.741, f32[16,1024]{1,0:T(8,128)S(1)} %get-tuple-element.739, pred[1024,512]{0,1:T(8,128)(4,1)S(1)} %copy-done.21, bf16[512,16,64]{0,2,1:T(8,128)(2,1)S(1)} %bitcast.349, ...), kind=kOutput, calls=%fused_computation.30.clone.1 | convolution fusion | flops 1115684864 | bytes 54132736 | tf_op jit(solution)/shard_map/while/body/eval_jaxpr/qhd,khd->hqk/dot_general | solution.py:244
  1305.6 13.2 fusion.198
  1318.9 15.4 fusion.200
  1334.3 20.7 %fusion.199 = bf16[16,1024,512]{1,2,0:T(8,128)(2,1)} fusion(f32[16,512,1024]{2,1,0:T(8,128)} %fusion.198, f32[16,1024]{1,0:T(8,128)S(1)} %get-tuple-element.741, f32[16,1024]{1,0:T(8,128)S(1)} %get-tuple-element.739, pred[1024,512]{0,1:T(8,128)(4,1)S(1)} %copy-done.21, bf16[512,16,64]{0,2,1:T(8,128)(2,1)S(1)} %bitcast.349, ...), kind=kOutput, calls=%fused_computation.30.clone.1 | convolution fusion | flops 1115684864 | bytes 54132736 | tf_op jit(solution)/shard_map/while/body/eval_jaxpr/qhd,khd->hqk/dot_general | solution.py:244
  1393.8 13.1 fusion.198
  1406.9 15.4 fusion.200
  1422.4 20.7 %fusion.199 = bf16[16,1024,512]{1,2,0:T(8,128)(2,1)} fusion(f32[16,512,1024]{2,1,0:T(8,128)} %fusion.198, f32[16,1024]{1,0:T(8,128)S(1)} %get-tuple-element.741, f32[16,1024]{1,0:T(8,128)S(1)} %get-tuple-element.739, pred[1024,512]{0,1:T(8,128)(4,1)S(1)} %copy-done.21, bf16[512,16,64]{0,2,1:T(8,128)(2,1)S(1)} %bitcast.349, ...), kind=kOutput, calls=%fused_computation.30.clone.1 | convolution fusion | flops 1115684864 | bytes 54132736 | tf_op jit(solution)/shard_map/while/body/eval_jaxpr/qhd,khd->hqk/dot_general | solution.py:244
  1515.7 24.1 %fusion.51 = f32[1,1024,2048]{2,1,0:T(8,128)} fusion(bf16[4096,2048]{1,0:T(8,128)(2,1)} %fusion.31, bf16[1,4096,1024]{2,1,0:T(8,128)(2,1)} %all-gather.17.cloned.1.call-done), kind=kOutput, calls=%fused_computation.84 | convolution fusion | flops 17179869184 | bytes 33554432 | tf_op jit(solution)/shard_map/erd,erh->edh/dot_general | solution.py:215
  1539.8 26.9 %fusion.54 = f32[1,2048,1024]{2,1,0:T(8,128)} fusion(bf16[1,4096,1024]{2,1,0:T(8,128)(2,1)} %all-gather.19.cloned.1.call-done, f32[4096,2048]{1,0:T(8,128)} %fusion.38), kind=kOutput, calls=%fused_computation.85 | convolution fusion | flops 17255366656 | bytes 50331648 | tf_op jit(solution)/shard_map/erh,erd->ehd/dot_general | solution.py:211
  1570.8 12.6 fusion.127
  1594.2 59.0 %all-reduce.8 = (f32[1024]{0:T(1024)S(1)}, f32[1024]{0:T(1024)S(1)}, f32[1024]{0:T(1024)S(1)}, f32[1024]{0:T(1024)S(1)}, f32[1024]{0:T(1024)S(1)}, /*index=5*/f3...) all-reduce(f32[1024]{0:T(1024)S(1)} %get-tuple-element.402, ...), channel_id=4, replica_groups=mesh['fsdp'=2,'expert'=16] {'fsdp','expert'}, use_global_device_ids=true, to_apply=%region_27.28.clone | all-reduce | flops 8192 | bytes 65536
  1668.1 18.3 %reduce-scatter.12.cloned.1.call-done = f32[32,3072]{1,0:T(8,128)} async-done(((f32[1024,3072]{1,0:T(8,128)}), f32[32,3072]{1,0:T(8,128)}) %reduce-scatter.12.cloned.1.call-update) | async-done | bytes 393232 | tf_op jit(solution)/shard_map/reduce_scatter | solution.py:286
  (453 shorter events, 493.9 us)
Async XLA Ops:
  7.2 21.9 %all-gather.13.cloned.1.call-start = ((), (), s32[]{:S(2)}) async-start(), calls=%async_computation.9 | async-start | bytes 9437184 | tf_op jit(solution)/shard_map/all_gather | solution.py:74
  7.9 285.7 %all-gather.15.cloned.1.call-start = ((), (), s32[]{:S(2)}) async-start(), calls=%async_computation.10 | async-start | bytes 3145728 | tf_op jit(solution)/shard_map/all_gather | solution.py:77
  10.6 18.5 %copy-start.49 = (f32[2,1,512]{2,1,0:T(1,128)}, f32[2,1,512]{2,1,0:T(1,128)S(1)}, u32[]{:S(2)}) copy-start(f32[2,1,512]{2,1,0:T(1,128)S(1)} %convert_element_type.200) | copy-start | bytes 12292
  13.0 16.0 copy-start.62
  21.0 17.3 %copy-start.7 = (bf16[1,1024,1024]{1,2,0:T(8,128)(2,1)}, bf16[1,1024,1024]{1,2,0:T(8,128)(2,1)S(1)}, u32[]{:S(2)}) copy-start(bf16[1,1024,1024]{1,2,0:T(8,128)(2,1)S(1)} %copy.127) | copy-start | bytes 6291460
  21.4 16.9 copy-start.38
  22.0 16.3 copy-start.51
  41.4 12.2 copy-start.68
  41.4 14.6 copy-start.69
  41.4 17.0 %copy-start.42 = (s32[1,1024,1]{1,2,0:T(1,128)S(1)}, s32[1,1024,1]{1,2,0:T(1,128)}, u32[]{:S(2)}) copy-start(s32[1,1024,1]{1,2,0:T(1,128)} %param.23) | copy-start | bytes 12292
  41.4 21.8 %copy-start.61 = (bf16[512,16]{0,1:T(8,128)(2,1)S(1)}, bf16[512,16]{0,1:T(8,128)(2,1)}, u32[]{:S(2)}) copy-start(bf16[512,16]{0,1:T(8,128)(2,1)} %param.34) | copy-start | bytes 49156
  44.1 24.8 %collective-permute-start = (bf16[1024,2048]{1,0:T(8,128)(2,1)}, bf16[1024,2048]{1,0:T(8,128)(2,1)}, u32[]{:S(2)}, u32[]{:S(2)}) collective-permute-start(bf16[1024,2048]{1,0:T(8,128)(2,1)} %pad_maximum_fusion.1), channel_id=1, source_target_pairs={{0,16},{1,17},{2,18},{3,19},{4,20},{5,21},{6,22},{7,23},{8,24},{9,... | collective-permute-start | bytes 12582920 | tf_op jit(solution)/shard_map/ppermute | solution.py:16
  48.2 385.6 %all-gather.17.cloned.1.call-start = ((), (), s32[]{:S(2)}) async-start(), calls=%async_computation.11 | async-start | bytes 12582912 | tf_op jit(solution)/shard_map/all_gather | solution.py:185
  288.6 10.5 copy-start.1
  288.6 10.5 copy-start.23
  304.8 110.6 %copy-start.40 = (f32[1024]{0:T(1024)}, f32[1024]{0:T(1024)S(1)}, u32[]{:S(2)}) copy-start(f32[1024]{0:T(1024)S(1)} %get-tuple-element.487) | copy-start | bytes 12292
  304.9 110.6 %copy-start.57 = (f32[1024]{0:T(1024)}, f32[1024]{0:T(1024)S(1)}, u32[]{:S(2)}) copy-start(f32[1024]{0:T(1024)S(1)} %fusion.110) | copy-start | bytes 12292
  415.5 89.9 %reduce-scatter.8.cloned.1.call-start = ((), (), s32[]{:S(2)}) async-start(), calls=%async_computation.12 | async-start | bytes 12582912 | tf_op jit(solution)/shard_map/reduce_scatter | solution.py:189
  433.9 25.7 %copy-start.73 = (bf16[1,2048,1024]{2,1,0:T(8,128)(2,1)S(1)}, bf16[1,2048,1024]{2,1,0:T(8,128)(2,1)}, u32[]{:S(2)}) copy-start(bf16[1,2048,1024]{2,1,0:T(8,128)(2,1)} %param.37) | copy-start | bytes 12582916
  552.0 87.4 %all-to-all-start.1 = ((bf16[16,2,65536]{2,1,0:T(2,128)(2,1)}), bf16[16,2,65536]{2,1,0:T(2,128)(2,1)}, u32[]{:S(2)}, u32[]{:S(2)}) async-start(bf16[16,2,65536]{2,1,0:T(2,128)(2,1)} %reshape.491), calls=%async_computation.2 | async-start | bytes 8388608 | tf_op jit(solution)/shard_map/all_to_all | solution.py:192
  559.0 287.1 %all-gather.19.cloned.1.call-start = ((), (), s32[]{:S(2)}) async-start(), calls=%async_computation.13 | async-start | bytes 12582912 | tf_op jit(solution)/shard_map/all_gather | solution.py:209
  561.9 121.7 %copy-start.12 = (bf16[1,1024,1024]{1,2,0:T(8,128)(2,1)}, bf16[1,1024,1024]{1,2,0:T(8,128)(2,1)S(1)}, u32[]{:S(2)}) copy-start(bf16[1,1024,1024]{1,2,0:T(8,128)(2,1)S(1)} %copy.135) | copy-start | bytes 6291460
  827.7 102.7 %reduce-scatter.10.cloned.1.call-start = ((), (), s32[]{:S(2)}) async-start(), calls=%async_computation.14 | async-start | bytes 12582912 | tf_op jit(solution)/shard_map/reduce_scatter | solution.py:217
  976.4 88.9 %all-to-all-start.3 = ((bf16[16,2,65536]{2,1,0:T(2,128)(2,1)}), bf16[16,2,65536]{2,1,0:T(2,128)(2,1)}, u32[]{:S(2)}, u32[]{:S(2)}) async-start(bf16[16,2,65536]{2,1,0:T(2,128)(2,1)} %reshape.493), calls=%async_computation.5 | async-start | bytes 8388608 | tf_op jit(solution)/shard_map/all_to_all | solution.py:221
  983.5 530.8 %reduce-scatter.16.cloned.1.call-start = ((), (), s32[]{:S(2)}) async-start(), calls=%async_computation.17 | async-start | bytes 540672
  987.0 681.1 %reduce-scatter.14.cloned.1.call-start = ((), (), s32[]{:S(2)}) async-start(), calls=%async_computation.16 | async-start | bytes 4325376 | tf_op jit(solution)/shard_map/reduce_scatter | solution.py:291
  1122.7 563.7 %reduce-scatter.12.cloned.1.call-start = ((), (), s32[]{:S(2)}) async-start(), calls=%async_computation.15 | async-start | bytes 12976128 | tf_op jit(solution)/shard_map/reduce_scatter | solution.py:286
  1124.4 35.3 %copy-start.36 = (f32[16,1024]{1,0:T(8,128)}, f32[16,1024]{1,0:T(8,128)S(1)}, u32[]{:S(2)}) copy-start(f32[16,1024]{1,0:T(8,128)S(1)} %get-tuple-element.741) | copy-start | bytes 196612 | tf_op jit(solution)/shard_map/while
  1124.4 35.3 %copy-start.45 = (f32[16,1024]{1,0:T(8,128)}, f32[16,1024]{1,0:T(8,128)S(1)}, u32[]{:S(2)}) copy-start(f32[16,1024]{1,0:T(8,128)S(1)} %get-tuple-element.739) | copy-start | bytes 196612 | tf_op jit(solution)/shard_map/while
  1144.3 15.5 copy-start.16
  1144.3 15.5 copy-start.21
  1180.5 12.0 copy-start
  1210.4 35.5 %copy-start.36 = (f32[16,1024]{1,0:T(8,128)}, f32[16,1024]{1,0:T(8,128)S(1)}, u32[]{:S(2)}) copy-start(f32[16,1024]{1,0:T(8,128)S(1)} %get-tuple-element.741) | copy-start | bytes 196612 | tf_op jit(solution)/shard_map/while
  1210.5 35.4 %copy-start.45 = (f32[16,1024]{1,0:T(8,128)}, f32[16,1024]{1,0:T(8,128)S(1)}, u32[]{:S(2)}) copy-start(f32[16,1024]{1,0:T(8,128)S(1)} %get-tuple-element.739) | copy-start | bytes 196612 | tf_op jit(solution)/shard_map/while
  1230.3 15.6 copy-start.16
  1230.3 15.6 copy-start.21
  1266.7 12.1 copy-start
  1299.0 35.3 %copy-start.36 = (f32[16,1024]{1,0:T(8,128)}, f32[16,1024]{1,0:T(8,128)S(1)}, u32[]{:S(2)}) copy-start(f32[16,1024]{1,0:T(8,128)S(1)} %get-tuple-element.741) | copy-start | bytes 196612 | tf_op jit(solution)/shard_map/while
  1299.0 35.3 %copy-start.45 = (f32[16,1024]{1,0:T(8,128)}, f32[16,1024]{1,0:T(8,128)S(1)}, u32[]{:S(2)}) copy-start(f32[16,1024]{1,0:T(8,128)S(1)} %get-tuple-element.739) | copy-start | bytes 196612 | tf_op jit(solution)/shard_map/while
  1318.9 15.5 copy-start.16
  1318.9 15.5 copy-start.21
  1355.0 11.9 copy-start
  1387.1 35.2 %copy-start.36 = (f32[16,1024]{1,0:T(8,128)}, f32[16,1024]{1,0:T(8,128)S(1)}, u32[]{:S(2)}) copy-start(f32[16,1024]{1,0:T(8,128)S(1)} %get-tuple-element.741) | copy-start | bytes 196612 | tf_op jit(solution)/shard_map/while
  1387.2 35.2 %copy-start.45 = (f32[16,1024]{1,0:T(8,128)}, f32[16,1024]{1,0:T(8,128)S(1)}, u32[]{:S(2)}) copy-start(f32[16,1024]{1,0:T(8,128)S(1)} %get-tuple-element.739) | copy-start | bytes 196612 | tf_op jit(solution)/shard_map/while
  1406.9 15.5 copy-start.16
  1406.9 15.5 copy-start.21
  1443.1 11.9 copy-start
  1481.6 12.5 collective-permute-start.1
  (70 other events, 376.0 us)
Sparse Core Ops, SparseCore 0:
  9.6 19.4 all-gather.12
  48.4 11.8 all-gather.14
  415.6 18.2 all-gather.16
  487.3 17.9 reduce-scatter.7
  827.8 18.2 all-gather.18
  912.4 17.9 reduce-scatter.9
  987.1 179.9 reduce-scatter.15
  1170.1 146.1 reduce-scatter.13
  1512.5 173.9 reduce-scatter.11
